TPU v7x, 256 devices: a whole 4x4x8 slice. The times are simulated.
256 devices in a mesh: cuts: 4 (over y), blk: 64 (over x, z, core).
Axes of the slice: x: 4, y: 4, z: 8, core: 2. Of those that a mesh axis runs over, the one named last changes fastest.
Arguments:
- gap_load: float32 [4, 128, 2, 256, 128], P('cuts', 'blk'), may hold values from -24 to 24
- offsets: int32 [4, 128, 2], P('cuts', 'blk'), may hold values from -1 to 255, as said below
- corner_map: int32 [4, 128, 4], P('cuts', 'blk'), may hold values from -1 to 511, as said below
- flexibility: float32 [4, 128, 1024, 1024], P('cuts', 'blk'), may hold values from -0.5 to 4.5, as said below
- coupling: float32 [4, 128, 12, 1024], P('cuts', 'blk'), may hold values from -1.25 to 1.25
- corner_rows: float32 [4, 128, 12, 1536], P('cuts', 'blk'), may hold values from -0.1 to 1.1, as said below
Outputs:
- multipliers: float32 [4, 128, 2, 256, 128], P('cuts', 'blk')
- residual: float32 [4, 128, 2, 256, 128], P('cuts', 'blk')
Inputs may be any that keep to these rules, and one draw needn't show every extreme that they name: `offsets`: on an interface owned by a subdomain, the neighbour's dof k matches the owner's dof (k + offset) mod 256; -1 marks an interface without multipliers: the tunnel's far end, or one that touches an excavated subdomain. `corner_map`: entries k = 0, 1, 2, 3 are the corners at near-left, near-right, far-left, far-right. Entry 2 of subdomain (r, c) is never -1, and every node is entry 2 of exactly one subdomain; the same node is entry 3 of (r, (c - 1) mod 128) and, for r + 1 < 4, entries 0 of (r + 1, c) and 1 of (r + 1, (c - 1) mod 128), and no other entry. -1 marks a clamped corner at the tunnel's near end. `flexibility`: each block is symmetric positive definite. `corner_rows`: row 3 k + j of a subdomain is row 3 m + j of one symmetric positive definite matrix of order 3 * 512, with m = corner_map entry k; zero rows where that entry is -1.
All inputs are finite; a program needn't handle non-finite values.
Results may differ from a plain program's by a relative error of at most 0.00021.
Values sent between devices are 32-bit elements; how exact they have to be, the bound alone decides.
A program may use at most 64 MiB of HBM per device.

v0:
```python
import jax
import jax.numpy as jnp
from jax import lax
from jax.sharding import PartitionSpec as P

ITERS = 3


HIGH = lax.Precision.HIGHEST


def from_behind(value, axis, steps):
    count = lax.axis_size(axis)
    first, last = (max(0, -steps), min(count, count - steps))
    return lax.ppermute(value, axis, [(source, source + steps) for source in range(first, last)])


def passed_along(value, axis, steps):
    count = lax.axis_size(axis)
    pairs = [(source, (source + steps) % count) for source in range(count)]
    return lax.ppermute(value, axis, pairs)


def rotate(values, amounts, orient):
    face_size = values.shape[-2]
    indices = (jnp.arange(face_size, dtype=jnp.int32) + orient * amounts[..., None]) % face_size
    return jnp.take_along_axis(values, indices[..., None], axis=-2)


def corner_indices(corner_map, dof_count):
    spread = 3 * corner_map[..., None] + jnp.arange(3, dtype=jnp.int32)
    spread = jnp.where(corner_map[..., None] >= 0, spread, dof_count)
    return spread.reshape(corner_map.shape[0], corner_map.shape[1], 12)


def inner_sum(first, second):
    return jnp.sum(first * second, axis=(0, 1, 2, 3))


def squares(residual):
    return lax.psum(inner_sum(residual, residual), ("cuts", "blk"))


def per_device(gap_load, offsets, corner_map, flexibility, coupling, corner_rows):
    cycle_count, circ_count, _, face_size, load_count = gap_load.shape
    dof_count = corner_rows.shape[-1]
    active = (offsets >= 0).astype(jnp.float32)[..., None, None]
    corner_dofs = corner_indices(corner_map, dof_count)
    residual = gap_load * active
    multipliers = jnp.zeros_like(residual)
    direction = residual
    norm_now = squares(residual)
    for iteration in range(ITERS):
        sent_far = -rotate(direction[:, :, 0], offsets[:, :, 0], 1)
        sent_right = -rotate(direction[:, :, 1], offsets[:, :, 1], 1)
        edge_near = from_behind(sent_far[-1], "cuts", 1)
        edge_left = passed_along(sent_right[:, -1], "blk", 1)
        nearside = jnp.concatenate([edge_near[None], sent_far[:-1]], axis=0)
        leftside = jnp.concatenate([edge_left[:, None], sent_right[:, :-1]], axis=1)
        loads = jnp.stack([nearside, direction[:, :, 0], leftside, direction[:, :, 1]], axis=2)
        loads = loads.reshape(cycle_count, circ_count, 4 * face_size, load_count)
        operator_corner_terms = jnp.einsum("rcki,rcin->rckn", coupling, loads, precision=HIGH)
        partial_value = jnp.zeros((dof_count, load_count), jnp.float32)
        partial_value = partial_value.at[corner_dofs.reshape(-1)].add(
            operator_corner_terms.reshape(-1, load_count), mode="drop"
        )
        coarse = lax.psum(partial_value, ("cuts", "blk"))
        corner_values = jnp.einsum("rckm,mn->rckn", corner_rows, coarse, precision=HIGH)
        moved = jnp.einsum("rcij,rcjn->rcin", flexibility, loads, precision=HIGH)
        moved = moved + jnp.einsum("rcki,rckn->rcin", coupling, corner_values, precision=HIGH)
        moved = moved.reshape(cycle_count, circ_count, 4, face_size, load_count)
        from_far = from_behind(moved[0, :, 0], "cuts", -1)
        from_right = passed_along(moved[:, 0, 2], "blk", -1)
        far_near = jnp.concatenate([moved[1:, :, 0], from_far[None]], axis=0)
        right_left = jnp.concatenate([moved[:, 1:, 2], from_right[:, None]], axis=1)
        jump_far = moved[:, :, 1] - rotate(far_near, offsets[:, :, 0], -1)
        jump_right = moved[:, :, 3] - rotate(right_left, offsets[:, :, 1], -1)
        mapped = jnp.stack([jump_far, jump_right], axis=2) * active
        step_size = norm_now / lax.psum(inner_sum(direction, mapped), ("cuts", "blk"))
        multipliers = multipliers + step_size * direction
        residual = residual - step_size * mapped
        norm_next = squares(residual)
        direction = residual + norm_next / norm_now * direction
        norm_now = norm_next
    return (multipliers, residual)


def solution(mesh):
    in_specs = (
        P("cuts", "blk", None, None, None),
        P("cuts", "blk", None),
        P("cuts", "blk", None),
        P("cuts", "blk", None, None),
        P("cuts", "blk", None, None),
        P("cuts", "blk", None, None),
    )
    out_specs = (P("cuts", "blk", None, None, None), P("cuts", "blk", None, None, None))
    return jax.shard_map(
        per_device, mesh=mesh, in_specs=in_specs, out_specs=out_specs, check_vma=False
    )
```

profile of v0, /device:TPU:1, one launch (start us, length us, event | category | flops | bytes accessed | tf_op | source)
XLA Modules:
  0.0 1306.6 jit_solution(7525697432891195552)
XLA Ops:
  8.0 1.0 multiply_reduce_fusion.7
  9.2 1.1 copy_multiply_fusion
  10.4 3.7 gather_fusion.1
  14.3 3.1 collective-permute-start.1
  17.6 3.7 gather_fusion
  21.4 3.2 collective-permute-start
  25.0 4.6 collective-permute-done
  30.7 1.0 convolution_bitcast_fusion.5
  31.7 1.6 scatter_custom_fusion
  33.4 11.0 fusion.4
  44.4 248.0 %all-reduce.5.cloned.1.call-done = f32[1536,128]{1,0:T(8,128)} async-done(((f32[1536,128]{1,0:T(8,128)}), f32[1536,128]{1,0:T(8,128)}) %all-reduce.5.cloned.1.call-update) | async-done | bytes 786448 | tf_op jit(solution)/shard_map/psum | solution.py:67
  292.4 1.8 convolution_bitcast_fusion.4
  294.2 2.0 fusion.8
  296.2 1.7 reshape.723
  298.3 2.4 collective-permute-start.3
  301.8 1.3 collective-permute-start.2
  303.1 3.7 gather_fusion.3
  306.9 2.0 collective-permute-done.2
  308.9 3.7 gather_fusion.2
  312.9 78.9 %all-reduce = (f32[128]{0:T(128)S(1)}, f32[128]{0:T(128)S(1)}) all-reduce(f32[128]{0:T(128)S(1)} %get-tuple-element.8, f32[128]{0:T(128)S(1)} %get-tuple-element.7), channel_id=1, replica_groups=mesh['cuts'=4,'blk'=64] {'cuts','blk'}, use_global_device_ids=true, to_apply=%region_1.2 | all-reduce | flops 256 | bytes 2048 | tf_op jit(solution)/shard_map/psum | solution.py:41
  392.0 72.6 %psum.66 = f32[128]{0:T(128)S(1)} all-reduce(f32[128]{0:T(128)S(1)} %multiply_reduce_fusion.3), channel_id=1, replica_groups=mesh['cuts'=4,'blk'=64] {'cuts','blk'}, use_global_device_ids=true, to_apply=%region_7.9 | all-reduce | flops 128 | bytes 1024 | tf_op jit(solution)/shard_map/psum | solution.py:41
  464.9 3.7 gather_fusion.4
  468.7 3.7 gather_fusion.5
  472.5 2.4 collective-permute-start.4
  475.0 2.7 collective-permute-start.5
  477.7 1.9 collective-permute-done.5
  481.0 1.0 convolution_bitcast_fusion.3
  482.0 1.6 scatter_custom_fusion.1
  483.9 11.0 fusion.2
  494.9 243.5 %all-reduce.7.cloned.1.call-done = f32[1536,128]{1,0:T(8,128)} async-done(((f32[1536,128]{1,0:T(8,128)}), f32[1536,128]{1,0:T(8,128)}) %all-reduce.7.cloned.1.call-update) | async-done | bytes 786448 | tf_op jit(solution)/shard_map/psum | solution.py:67
  738.4 1.7 convolution_bitcast_fusion.2
  740.1 2.0 fusion.7
  742.1 1.7 reshape.726
  744.9 2.2 collective-permute-start.7
  748.1 1.3 collective-permute-start.6
  750.5 3.7 gather_fusion.7
  755.2 3.7 gather_fusion.6
  759.9 80.2 %psum.68 = f32[128]{0:T(128)S(1)} all-reduce(f32[128]{0:T(128)S(1)} %multiply_reduce_fusion.2), channel_id=1, replica_groups=mesh['cuts'=4,'blk'=64] {'cuts','blk'}, use_global_device_ids=true, to_apply=%region_11.13 | all-reduce | flops 128 | bytes 1024 | tf_op jit(solution)/shard_map/psum | solution.py:79
  840.9 72.8 %psum.69 = f32[128]{0:T(128)S(1)} all-reduce(f32[128]{0:T(128)S(1)} %get-tuple-element.15), channel_id=1, replica_groups=mesh['cuts'=4,'blk'=64] {'cuts','blk'}, use_global_device_ids=true, to_apply=%region_13.15 | all-reduce | flops 128 | bytes 1024 | tf_op jit(solution)/shard_map/psum | solution.py:41
  915.3 3.7 gather_fusion.8
  919.8 3.7 gather_fusion.9
  923.6 2.2 collective-permute-start.8
  925.8 2.7 collective-permute-start.9
  928.5 1.9 collective-permute-done.9
  930.8 1.3 copy.59
  932.2 1.8 reshape.727
  934.0 1.0 convolution_bitcast_fusion.1
  935.0 1.7 scatter_custom_fusion.2
  936.7 12.0 fusion
  948.8 242.0 %all-reduce.9.cloned.1.call-done = f32[1536,128]{1,0:T(8,128)} async-done(((f32[1536,128]{1,0:T(8,128)}), f32[1536,128]{1,0:T(8,128)}) %all-reduce.9.cloned.1.call-update) | async-done | bytes 786448 | tf_op jit(solution)/shard_map/psum | solution.py:67
  1190.8 1.7 convolution_bitcast_fusion
  1192.5 3.3 fusion.6
  1195.8 1.7 reshape.729
  1198.5 1.7 copy.88
  1200.1 2.3 collective-permute-start.11
  1202.4 1.5 fusion.46
  1203.9 1.8 copy.85
  1205.7 1.8 copy.86
  1207.5 1.1 copy.84
  1208.6 1.3 collective-permute-start.10
  1210.8 3.7 gather_fusion.11
  1214.5 1.1 fusion.18
  1215.9 3.7 gather_fusion.10
  1220.0 77.9 %psum.71 = f32[128]{0:T(128)S(1)} all-reduce(f32[128]{0:T(128)S(1)} %multiply_reduce_fusion), channel_id=1, replica_groups=mesh['cuts'=4,'blk'=64] {'cuts','blk'}, use_global_device_ids=true, to_apply=%region_17.19 | all-reduce | flops 128 | bytes 1024 | tf_op jit(solution)/shard_map/psum | solution.py:79
  (129 shorter events, 21.0 us)
Async XLA Ops:
  7.2 285.2 %copy-start = (f32[1,2,12,1536]{3,1,2,0:T(2,128)S(1)}, f32[1,2,12,1536]{3,1,2,0:T(2,128)}, u32[]{:S(2)}) copy-start(f32[1,2,12,1536]{3,1,2,0:T(2,128)} %param.13) | copy-start | bytes 442372
  7.2 17.4 %copy-start.12 = (s32[1,2,4]{2,1,0:T(2,128)S(1)}, s32[1,2,4]{2,1,0:T(2,128)}, u32[]{:S(2)}) copy-start(s32[1,2,4]{2,1,0:T(2,128)} %param.10) | copy-start | bytes 100
  7.2 23.5 %copy-start.2 = (f32[1,2,12,1024]{3,1,2,0:T(2,128)S(1)}, f32[1,2,12,1024]{3,1,2,0:T(2,128)}, u32[]{:S(2)}) copy-start(f32[1,2,12,1024]{3,1,2,0:T(2,128)} %param.12) | copy-start | bytes 294916
  7.2 285.2 %all-reduce.5.cloned.1.call-start = ((), (), s32[]{:S(2)}) async-start(), calls=%async_computation | async-start | bytes 1572864 | tf_op jit(solution)/shard_map/psum | solution.py:67
  9.0 463.4 %copy-start.5 = (pred[2,256]{1,0:T(4,128)(4,1)}, pred[2,256]{1,0:T(4,128)(4,1)S(1)}, u32[]{:S(2)}) copy-start(pred[2,256]{1,0:T(4,128)(4,1)S(1)} %and_bitcast_fusion.2) | copy-start | bytes 1540
  14.3 10.7 collective-permute-start.1
  17.5 451.1 %copy-start.7 = (pred[2,256]{1,0:T(4,128)(4,1)}, pred[2,256]{1,0:T(4,128)(4,1)S(1)}, u32[]{:S(2)}) copy-start(pred[2,256]{1,0:T(4,128)(4,1)S(1)} %and_bitcast_fusion.3) | copy-start | bytes 1540
  21.4 8.3 collective-permute-start
  25.0 457.0 %copy-start.13 = (s32[24]{0:T(128)}, s32[24]{0:T(128)S(1)}, u32[]{:S(2)}) copy-start(s32[24]{0:T(128)S(1)} %fusion.45) | copy-start | bytes 292
  33.3 705.1 %all-reduce.7.cloned.1.call-start = ((), (), s32[]{:S(2)}) async-start(), calls=%async_computation.1 | async-start | bytes 1572864 | tf_op jit(solution)/shard_map/psum | solution.py:67
  292.4 20.3 %copy-start.1 = (f32[1,2,2,256,128]{4,3,2,1,0:T(8,128)S(1)}, f32[1,2,2,256,128]{4,3,2,1,0:T(8,128)}, u32[]{:S(2)}) copy-start(f32[1,2,2,256,128]{4,3,2,1,0:T(8,128)} %param.8) | copy-start | bytes 1572868
  298.3 4.8 collective-permute-start.3
  301.8 7.1 collective-permute-start.2
  464.6 16.3 %copy-start.14 = (f32[128]{0:T(128)}, f32[128]{0:T(128)S(1)}, u32[]{:S(2)}) copy-start(f32[128]{0:T(128)S(1)} %psum.66) | copy-start | bytes 1540
  464.6 16.3 %copy-start.8 = (f32[128]{0:T(128)}, f32[128]{0:T(128)S(1)}, u32[]{:S(2)}) copy-start(f32[128]{0:T(128)S(1)} %div.16) | copy-start | bytes 1540
  472.5 7.4 collective-permute-start.4
  475.0 4.6 collective-permute-start.5
  483.6 707.2 %all-reduce.9.cloned.1.call-start = ((), (), s32[]{:S(2)}) async-start(), calls=%async_computation.2 | async-start | bytes 1572864 | tf_op jit(solution)/shard_map/psum | solution.py:67
  744.9 4.7 collective-permute-start.7
  748.1 7.1 collective-permute-start.6
  755.2 168.2 %copy-start.6 = (pred[2,256]{1,0:T(4,128)(4,1)S(1)}, pred[2,256]{1,0:T(4,128)(4,1)}, u32[]{:S(2)}) copy-start(pred[2,256]{1,0:T(4,128)(4,1)} %copy-done.5) | copy-start | bytes 1540
  840.7 91.5 %copy-start.10 = (f32[128]{0:T(128)}, f32[128]{0:T(128)S(1)}, u32[]{:S(2)}) copy-start(f32[128]{0:T(128)S(1)} %div.17) | copy-start | bytes 1540
  840.9 73.4 %copy-start.3 = (f32[1,2,2,256,128]{4,3,1,2,0:T(8,128)}, f32[1,2,2,256,128]{4,3,1,2,0:T(8,128)S(1)}, u32[]{:S(2)}) copy-start(f32[1,2,2,256,128]{4,3,1,2,0:T(8,128)S(1)} %get-tuple-element.16) | copy-start | bytes 1572868
  913.7 20.2 %copy-start.15 = (f32[128]{0:T(128)}, f32[128]{0:T(128)S(1)}, u32[]{:S(2)}) copy-start(f32[128]{0:T(128)S(1)} %psum.69) | copy-start | bytes 1540
  923.6 7.2 collective-permute-start.8
  925.8 4.6 collective-permute-start.9
  1192.5 105.4 %copy-start.4 = (f32[1,2,2,256,128]{4,3,1,2,0:T(8,128)S(1)}, f32[1,2,2,256,128]{4,3,1,2,0:T(8,128)}, u32[]{:S(2)}) copy-start(f32[1,2,2,256,128]{4,3,1,2,0:T(8,128)} %copy-done.3) | copy-start | bytes 1572868
  1192.5 105.4 %copy-start.9 = (f32[128]{0:T(128)S(1)}, f32[128]{0:T(128)}, u32[]{:S(2)}) copy-start(f32[128]{0:T(128)} %copy-done.8) | copy-start | bytes 1540
  1192.5 105.4 %copy-start.11 = (f32[128]{0:T(128)S(1)}, f32[128]{0:T(128)}, u32[]{:S(2)}) copy-start(f32[128]{0:T(128)} %copy-done.10) | copy-start | bytes 1540
  1195.8 102.1 %copy-start.16 = (f32[128]{0:T(128)S(1)}, f32[128]{0:T(128)}, u32[]{:S(2)}) copy-start(f32[128]{0:T(128)} %copy-done.15) | copy-start | bytes 1540
  1200.1 9.8 collective-permute-start.11
  1208.6 7.3 collective-permute-start.10
Sparse Core Ops, SparseCore 0:
  33.4 258.9 all-reduce.4
  483.7 254.6 all-reduce.6
  936.8 253.8 all-reduce.8
where the time goes:
time: 1320 us; the launch traced here: 1310 us
  waiting for transfers between devices  746 us (57%)
  blocking collectives  382 us (29%)
  local copies, waits for them, and re-layouts  68.4 us (5%)
  matrix products  49.6 us (4%)
  starting transfers between devices  27.4 us (2%)
  other arithmetic  18.2 us (1%)
  between operations  14.7 us (1%)
    psum x3, waiting for transfers between devices, per_device(): coarse = lax.psum(partial_value, ('cuts', 'blk'))  733 us
    psum x3, blocking collectives, squares(): return lax.psum(inner_sum(residual, residual), ('cuts', 'blk'))  224 us
    psum x2, blocking collectives, per_device(): lax.psum(inner_sum(direction, mapped), ('cuts', 'blk'))  158 us
    gather x12, local copies, waits for them, and re-layouts, rotate(): return jnp.take_along_axis(values, indices[..., None], axis=-2)  43.9 us
    dot_general x3, matrix products, per_device(): moved = jnp.einsum('rcij,rcjn->rcin', flexibility, loads, precision=HIGH)  34.1 us
  transfers between devices with their start and end apart: 15, of which 12 were waited for; matrix products, arithmetic and copies ran while one was open for 5% of the time, Pallas kernels for 0%

commit v1 on v0

v1 whole, which is shorter than its diff:
```python
import functools

import jax
import jax.numpy as jnp
from jax import lax
from jax.experimental import pallas as pl
from jax.experimental.pallas import tpu as pltpu
from jax.sharding import PartitionSpec as P

MESH = pl.DeviceIdType.MESH
F32, BF16 = jnp.float32, jnp.bfloat16
FD, RHS = 256, 128
NEAR, FAR, LEFT, RIGHT = 0, 1, 2, 3
BLOCK = 40
APPS = 3


def halves(value):
    high = value.astype(BF16)
    return high, (value - high.astype(F32)).astype(BF16)


def quadrants(product):
    rows = product.shape[0] // 2
    wide = product[:rows] + product[rows:]
    return wide[:, :RHS] + wide[:, RHS:]


def face(index):
    return slice(index * FD, (index + 1) * FD)


def scratch(ny, nx, nz, dofs):
    dma = pltpu.SemaphoreType.DMA
    rounds = APPS + 1
    return dict(
        stage=pltpu.VMEM((4, FD, 4 * FD), F32),
        flex_parts=pltpu.VMEM((2, 2, 4 * FD, 4 * FD), BF16),
        info=pltpu.VMEM((8, 128), jnp.int32),
        info_near=pltpu.VMEM((8, 128), jnp.int32),
        info_left=pltpu.VMEM((8, 128), jnp.int32),
        word_near=pltpu.SMEM((8, 128), jnp.int32),
        word_left=pltpu.SMEM((8, 128), jnp.int32),
        coup_pad=pltpu.VMEM((128, 4 * FD), F32),
        coup_t=pltpu.VMEM((2, 4 * FD, 128), BF16),
        coup_t_n=pltpu.VMEM((6, FD, 128), BF16),
        coup_far=pltpu.VMEM((2, 12, FD), F32),
        coup_near=pltpu.VMEM((2, 12, FD), F32),
        coup_left=pltpu.VMEM((12, FD), F32),
        coup_right=pltpu.VMEM((12, FD), F32),
        node_pad=pltpu.VMEM((32, 4 * FD), F32),
        node_rows=pltpu.VMEM((2, 64, 4 * FD), BF16),
        rows_mate=pltpu.VMEM((2, 12, dofs), F32),
        rows_pad=pltpu.VMEM((64, dofs), F32),
        rows_parts=pltpu.VMEM((128, dofs), BF16),
        pick=pltpu.VMEM((nz * BLOCK, dofs), BF16),
        coarse=pltpu.VMEM((nx, 128, nz * BLOCK), BF16),
        line=pltpu.VMEM((rounds, ny, 32, RHS), F32),
        blocks=pltpu.VMEM((rounds, nx, nz, BLOCK, RHS), F32),
        gap_near=pltpu.VMEM((2, FD, RHS), F32),
        gap_left=pltpu.VMEM((FD, RHS), F32),
        vec=pltpu.VMEM((5, 2, 4 * FD, RHS), F32),
        split=pltpu.VMEM((2, 4 * FD, 2 * RHS), BF16),
        moved=pltpu.VMEM((APPS, 2, 4 * FD, RHS), F32),
        total=pltpu.VMEM((2, 4 * FD, RHS), F32),
        face_far=pltpu.VMEM((APPS, 2, FD, RHS), F32),
        face_near=pltpu.VMEM((APPS, 2, FD, RHS), F32),
        face_left=pltpu.VMEM((APPS, FD, RHS), F32),
        face_right=pltpu.VMEM((APPS, FD, RHS), F32),
        twice=pltpu.VMEM((8, 2 * FD, RHS), F32),
        mate_out=pltpu.VMEM((APPS, 40, RHS), F32),
        mate_in=pltpu.VMEM((APPS, 40, RHS), F32),
        y_own=pltpu.VMEM((APPS, 2, 16, RHS), F32),
        y_far=pltpu.VMEM((APPS, 2, 16, RHS), F32),
        y_near=pltpu.VMEM((APPS, 2, 16, RHS), F32),
        y_left=pltpu.VMEM((APPS, 16, RHS), F32),
        y_right=pltpu.VMEM((APPS, 16, RHS), F32),
        own=pltpu.VMEM((6, 2, 2, FD, RHS), F32),
        end_y=pltpu.VMEM((ny, 8, RHS), F32),
        end_z=pltpu.VMEM((nz, 8, RHS), F32),
        end_x=pltpu.VMEM((nx, 8, RHS), F32),
        end_out=pltpu.VMEM((8, RHS), F32),
        end_in=pltpu.VMEM((8, RHS), F32),
        stage_sem=dma((4,)),
        word_sem=dma((2,)),
        setup_sem=dma((2, 10)),
        y_sem=dma((2, rounds, ny - 1)),
        z_sem=dma((2, rounds, nz - 1)),
        x_sem=dma((2, rounds, nx - 1, nz)),
        face_sem=dma((2, APPS, 4)),
        mate_sem=dma((2, APPS)),
        yv_sem=dma((2, APPS, 4)),
        end_sem=dma((2, ny + nx + nz - 2)),
    )


def kernel(ny, nx, nz, names, gap, offs, cmap, coup, rows, flex, mult_out, res_out, *refs):
    s = dict(zip(names, refs))
    y, b = lax.axis_index("cuts"), lax.axis_index("blk")
    nb = 2 * nx * nz
    k = lax.rem(b, 2)
    z = lax.rem(b // 2, nz)
    x = b // (2 * nz)
    at = lambda xx, zz, kk: (xx * nz + zz) * 2 + kk
    up, down = lax.rem(y + 1, ny), lax.rem(y + ny - 1, ny)
    right, left = lax.rem(b + 1, nb), lax.rem(b + nb - 1, nb)
    mate = at(x, z, 1 - k)
    y_peers = [(lax.rem(y + d, ny), b) for d in range(1, ny)]
    z_peers = [(y, at(x, lax.rem(z + d, nz), k)) for d in range(1, nz)]
    x_peers = [(y, at(lax.rem(x + d, nx), z, k)) for d in range(1, nx)]
    started = []

    def send(src, dst, sems, index, peer):
        copy = pltpu.make_async_remote_copy(
            src_ref=src,
            dst_ref=dst,
            send_sem=sems.at[(0,) + index],
            recv_sem=sems.at[(1,) + index],
            device_id=peer,
            device_id_type=MESH,
        )
        copy.start()
        started.append(copy)
        return copy

    def fetch(chunk):
        sub, part = divmod(chunk, 4)
        return pltpu.make_async_copy(
            flex.at[0, sub, face(part), :], s["stage"].at[chunk % 4], s["stage_sem"].at[chunk % 4]
        )

    for chunk in range(4):
        fetch(chunk).start()

    greeted = y_peers + z_peers + x_peers + [(y, right), (y, left)]
    barrier = pltpu.get_barrier_semaphore()
    for peer in greeted:
        pl.semaphore_signal(barrier, inc=1, device_id=peer, device_id_type=MESH)

    row = lax.broadcasted_iota(jnp.int32, (16, RHS), 0)
    slot = jnp.where(row < 3, 0, jnp.where(row < 6, 1, 2))
    node = jnp.where(row < 3, cmap[0, 0, 2], jnp.where(row < 6, cmap[0, 1, 2], cmap[0, 1, 3]))
    number = jnp.where(row < 9, 3 * node + row - 3 * slot, -1).astype(F32)
    s["line"][0, y] = jnp.concatenate([number, jnp.full((16, RHS), -1.0, F32)], axis=0)
    row8 = lax.broadcasted_iota(jnp.int32, (8, 128), 0)
    s["info"][...] = jnp.where(row8 == 0, offs[0, 0, 0], jnp.where(row8 == 1, offs[0, 1, 0], offs[0, 1, 1]))

    pl.semaphore_wait(barrier, len(greeted))

    def line_sends(rd):
        return [
            send(s["line"].at[rd, y], s["line"].at[rd, y], s["y_sem"], (rd, d), peer)
            for d, peer in enumerate(y_peers)
        ]

    def block_sends(rd):
        own = s["blocks"].at[rd, x, z]
        zs = [send(own, own, s["z_sem"], (rd, d), peer) for d, peer in enumerate(z_peers)]
        xs = [send(own, own, s["x_sem"], (rd, d, 0), peer) for d, peer in enumerate(x_peers)]
        return zs, xs

    order = sorted(range(1, nz), key=lambda d: min(d, nz - d))

    def forward(rd, zs):
        xs = []
        for d in order:
            zs[d - 1].wait_recv()
            got = s["blocks"].at[rd, x, lax.rem(z + nz - d, nz)]
            xs += [send(got, got, s["x_sem"], (rd, e, d), peer) for e, peer in enumerate(x_peers)]
        return xs

    number_line = line_sends(0)
    setup = s["setup_sem"]
    got_gap_near = send(gap.at[0, :, 0], s["gap_near"], setup, (0,), (up, b))
    got_gap_left = send(gap.at[0, 1, 1], s["gap_left"], setup, (1,), (y, right))
    got_info_near = send(s["info"], s["info_near"], setup, (2,), (up, b))
    got_info_left = send(s["info"], s["info_left"], setup, (3,), (y, right))
    got_rows = send(rows.at[0], s["rows_mate"], setup, (4,), (y, mate))
    got_coup = [
        send(coup.at[0, :, :, face(NEAR)], s["coup_far"], setup, (5,), (down, b)),
        send(coup.at[0, :, :, face(FAR)], s["coup_near"], setup, (6,), (up, b)),
        send(coup.at[0, 1, :, face(RIGHT)], s["coup_left"], setup, (7,), (y, right)),
        send(coup.at[0, 0, :, face(LEFT)], s["coup_right"], setup, (8,), (y, left)),
    ]

    not_first = jnp.where(y > 0, 1.0, 0.0).astype(F32)
    not_last = jnp.where(y < ny - 1, 1.0, 0.0).astype(F32)
    for sub in range(2):
        s["node_pad"][...] = jnp.zeros((32, 4 * FD), F32)
        s["node_pad"][3 * sub : 3 * sub + 6] = coup[0, sub, 6:12]
        s["node_pad"][16 + 3 * sub : 22 + 3 * sub] = coup[0, sub, 0:6] * not_first
        high, low = halves(s["node_pad"][...])
        s["node_rows"][sub, 0:32] = high
        s["node_rows"][sub, 32:64] = low

    def transposed(value):
        width = value.shape[1]
        pad = s["coup_pad"]
        high = value.astype(BF16).astype(F32)
        low = value - high
        pad[:, 0:width] = jnp.zeros((128, width), F32)
        pad[0:12, 0:width] = high
        pad[16:28, 0:width] = low
        pad[32:44, 0:width] = high
        pad[48:60, 0:width] = low
        return pad[:, 0:width].T.astype(BF16)

    for sub in range(2):
        s["coup_t"][sub] = transposed(coup[0, sub])

    def make_block(rd):
        own = s["blocks"].at[rd, x, z]
        for cycle in range(ny):
            value = s["line"][rd, cycle, 0:9]
            if rd > 0 and cycle + 1 < ny:
                value = value + s["line"][rd, cycle + 1, 16:25]
            own[9 * cycle : 9 * cycle + 9] = value
        if rd > 0:
            sums = s["line"][rd, 0, 9:13]
            for cycle in range(1, ny):
                sums = sums + s["line"][rd, cycle, 9:13]
        else:
            sums = jnp.full((4, RHS), -1.0, F32)
        own[9 * ny : 9 * ny + 4] = sums
        if 9 * ny + 4 < BLOCK:
            own[9 * ny + 4 : BLOCK] = jnp.full((BLOCK - 9 * ny - 4, RHS), -1.0, F32)

    for copy in number_line:
        copy.wait_recv()
    make_block(0)
    number_z, number_x = block_sends(0)

    def rolled(index, value, start):
        s["twice"][index, 0:FD] = value
        s["twice"][index, FD : 2 * FD] = value
        return s["twice"][index, pl.ds(start, FD)]

    ahead = lambda off: lax.rem(off + FD, FD)
    back = lambda off: lax.rem(FD - off, FD)
    on = lambda off: jnp.where(off >= 0, 1.0, 0.0).astype(F32)
    got_info_near.wait_recv()
    got_info_left.wait_recv()
    words = [
        pltpu.make_async_copy(s["info_near"], s["word_near"], s["word_sem"].at[0]),
        pltpu.make_async_copy(s["info_left"], s["word_left"], s["word_sem"].at[1]),
    ]
    for copy in words:
        copy.start()
    for copy in words:
        copy.wait()
    off_far = [offs[0, sub, 0] for sub in range(2)]
    off_right = [offs[0, sub, 1] for sub in range(2)]
    off_near = [s["word_near"][sub, 0] for sub in range(2)]
    off_left = s["word_left"][2, 0]
    on_far = [on(off) for off in off_far]
    on_right = [on(off) for off in off_right]
    on_near = [on(off) * not_first for off in off_near]
    on_left = on(off_left)

    for chunk in range(8):
        sub, part = divmod(chunk, 4)
        fetch(chunk).wait()

        @pl.loop(0, FD // 32)
        def _(step):
            at_row = pl.multiple_of(step * 32, 32)
            high, low = halves(s["stage"][chunk % 4, pl.ds(at_row, 32)])
            base = FD * (part % 2)
            s["flex_parts"][sub, part // 2, pl.ds(base + at_row, 32)] = high
            s["flex_parts"][sub, part // 2, pl.ds(2 * FD + base + at_row, 32)] = low

        if chunk + 4 < 8:
            fetch(chunk + 4).start()

    got_gap_near.wait_recv()
    got_gap_left.wait_recv()
    r0, w0, q0, w1, q1 = (s["vec"].at[i] for i in range(5))
    for sub in range(2):
        r0[sub, face(FAR)] = gap[0, sub, 0] * on_far[sub]
        r0[sub, face(RIGHT)] = gap[0, sub, 1] * on_right[sub]
        r0[sub, face(NEAR)] = rolled(sub, s["gap_near"][sub], ahead(off_near[sub])) * -on_near[sub]
    r0[0, face(LEFT)] = rolled(2, s["gap_left"][...], ahead(off_left)) * -on_left
    r0[1, face(LEFT)] = rolled(3, gap[0, 0, 1], ahead(off_right[0])) * -on_right[0]

    owned = [(sub, part) for sub in range(2) for part in range(2)]

    def dot(first, second):
        total = None
        for sub, part in owned:
            term = jnp.sum(first(sub, part) * second(sub, part), axis=0, keepdims=True)
            total = term if total is None else total + term
        return total

    def of(vector):
        return lambda sub, part: vector[sub, face(2 * part + 1)]

    def product(sub, group):
        wide = jnp.dot(s["flex_parts"][sub, group], s["split"][sub], preferred_element_type=F32)
        s["moved"][app, sub, 2 * FD * group : 2 * FD * (group + 1)] = quadrants(wide)

    def stacked(value):
        high, low = halves(value)
        return jnp.concatenate([high, high, low, low, jnp.zeros((64, RHS), BF16)], axis=0)

    def begin(vector, dots):
        rd = app + 1
        for sub in range(2):
            high, low = halves(vector[sub])
            s["split"][sub, :, 0:RHS] = high
            s["split"][sub, :, RHS : 2 * RHS] = low
        wide = jnp.dot(s["node_rows"][0], s["split"][0], preferred_element_type=F32)
        wide = wide + jnp.dot(s["node_rows"][1], s["split"][1], preferred_element_type=F32)
        tile = s["line"].at[rd, y]
        tile[...] = quadrants(wide)
        tile[9:11] = jnp.concatenate(dots, axis=0)
        return line_sends(rd)

    def finish_faces(result, last):
        moved = s["total"]
        for sub in range(2):
            term = jnp.dot(s["coup_t"][sub], stacked(s["y_own"][app, sub]), preferred_element_type=F32)
            moved[sub] = s["moved"][app, sub] + term

        def other(index, value, y_value):
            return value + jnp.dot(s["coup_t_n"][index], stacked(y_value), preferred_element_type=F32)

        inner_left, inner_right = moved[1, face(LEFT)], moved[0, face(RIGHT)]
        result[0, face(RIGHT)] = (inner_right - rolled(0, inner_left, back(off_right[0]))) * on_right[0]
        if not last:
            result[1, face(LEFT)] = (inner_left - rolled(1, inner_right, ahead(off_right[0]))) * on_right[0]
        for copy in got_y:
            copy.wait_recv()
        for copy in got_faces:
            copy.wait_recv()
        for sub in range(2):
            value = other(sub, s["face_far"][app, sub], s["y_far"][app, sub]) * not_last
            jump = moved[sub, face(FAR)] - rolled(2 + sub, value, back(off_far[sub]))
            result[sub, face(FAR)] = jump * on_far[sub]
            if not last:
                value = other(2 + sub, s["face_near"][app, sub], s["y_near"][app, sub])
                jump = moved[sub, face(NEAR)] - rolled(4 + sub, value, ahead(off_near[sub]))
                result[sub, face(NEAR)] = jump * on_near[sub]
        value = other(5, s["face_right"][app], s["y_right"][app])
        jump = moved[1, face(RIGHT)] - rolled(6, value, back(off_right[1]))
        result[1, face(RIGHT)] = jump * on_right[1]
        if not last:
            value = other(4, s["face_left"][app], s["y_left"][app])
            jump = moved[0, face(LEFT)] - rolled(7, value, ahead(off_left))
            result[0, face(LEFT)] = jump * on_left

    def update(target, base, factor, step):
        for sub in range(2):
            for part in range(4):
                target[sub, face(part)] = base[sub, face(part)] + factor * step[sub, face(part)]

    none = jnp.zeros((1, RHS), F32)
    r1, p1, x2, r2, s1, w2 = (s["own"].at[i] for i in range(6))
    plain = lambda vector: lambda sub, part: vector[sub, part]
    gamma, delta = [], []
    for app in range(APPS):
        last = app == APPS - 1
        if app == 0:
            vector, result, dots = r0, w0, [dot(of(r0), of(r0)), none]
        elif app == 1:
            vector, result, dots = w0, q0, [none, dot(of(r0), of(w0))]
        else:
            vector, result = w1, q1
            dots = [dot(plain(r1), plain(r1)), dot(plain(r1), of(w1))]
        got_line = begin(vector, dots)
        moved = s["moved"].at[app]
        for sub in range(2):
            product(sub, 0)
        got_faces = [send(moved.at[:, face(NEAR)], s["face_far"].at[app], s["face_sem"], (app, 0), (down, b))]
        if not last:
            got_faces.append(
                send(moved.at[:, face(FAR)], s["face_near"].at[app], s["face_sem"], (app, 1), (up, b))
            )
        if app == 0:
            number_x += forward(0, number_z)
        for copy in got_line:
            copy.wait_recv()
        make_block(app + 1)
        got_z, got_x = block_sends(app + 1)
        for sub in range(2):
            product(sub, 1)
        got_faces.append(
            send(moved.at[0, face(LEFT)], s["face_right"].at[app], s["face_sem"], (app, 2), (y, left))
        )
        if not last:
            got_faces.append(
                send(moved.at[1, face(RIGHT)], s["face_left"].at[app], s["face_sem"], (app, 3), (y, right))
            )
        if app == 0:
            got_rows.wait_recv()
            s["rows_pad"][...] = jnp.zeros(s["rows_pad"].shape, F32)
            for sub in range(2):
                s["rows_pad"][16 * sub : 16 * sub + 12] = rows[0, sub]
                s["rows_pad"][32 + 16 * sub : 44 + 16 * sub] = s["rows_mate"][sub]
            high, low = halves(s["rows_pad"][...])
            s["rows_parts"][0:64] = high
            s["rows_parts"][64:128] = low
            for copy in number_x:
                copy.wait_recv()
            dofs = s["pick"].shape[1]
            for xx in range(nx):
                numbers = s["blocks"][0, xx].reshape(nz * BLOCK, RHS)
                for q in range(dofs // 128):
                    lane = (lax.broadcasted_iota(jnp.int32, numbers.shape, 1) + 128 * q).astype(F32)
                    s["pick"][:, 128 * q : 128 * q + 128] = jnp.where(numbers == lane, 1.0, 0.0).astype(BF16)
                picked = lax.dot_general(
                    s["rows_parts"][...],
                    s["pick"][...],
                    (((1,), (1,)), ((), ())),
                    preferred_element_type=F32,
                )
                s["coarse"][xx] = picked.astype(BF16)
            for copy in got_coup:
                copy.wait_recv()
            for sub in range(2):
                s["coup_t_n"][sub] = transposed(s["coup_far"][sub])
                s["coup_t_n"][2 + sub] = transposed(s["coup_near"][sub])
            s["coup_t_n"][4] = transposed(s["coup_left"][...])
            s["coup_t_n"][5] = transposed(s["coup_right"][...])
        got_x += forward(app + 1, got_z)
        for copy in got_x:
            copy.wait_recv()
        wide = None
        sums = None
        for xx in range(nx):
            loads = s["blocks"][app + 1, xx]
            part = jnp.sum(loads[:, BLOCK - 8 :, :], axis=0)
            sums = part if sums is None else sums + part
            high, low = halves(loads.reshape(nz * BLOCK, RHS))
            term = jnp.dot(
                s["coarse"][xx], jnp.concatenate([high, low], axis=1), preferred_element_type=F32
            )
            wide = term if wide is None else wide + term
        ysum = quadrants(wide)
        s["mate_out"][app, 0:32] = ysum[32:64]
        s["mate_out"][app, 32:40] = sums
        mate_copy = send(s["mate_out"].at[app], s["mate_in"].at[app], s["mate_sem"], (app,), (y, mate))
        mate_copy.wait_recv()
        sums = sums + s["mate_in"][app, 32:40]
        for sub in range(2):
            s["y_own"][app, sub] = ysum[16 * sub : 16 * sub + 16] + s["mate_in"][app, 16 * sub : 16 * sub + 16]
        y_own = s["y_own"].at[app]
        got_y = [
            send(y_own, s["y_far"].at[app], s["yv_sem"], (app, 0), (down, b)),
            send(y_own.at[0], s["y_right"].at[app], s["yv_sem"], (app, 2), (y, left)),
        ]
        if not last:
            got_y += [
                send(y_own, s["y_near"].at[app], s["yv_sem"], (app, 1), (up, b)),
                send(y_own.at[1], s["y_left"].at[app], s["yv_sem"], (app, 3), (y, right)),
            ]
        finish_faces(result, last)
        first_row = 9 * ny - (BLOCK - 8)
        if app == 0:
            gamma.append(sums[first_row : first_row + 1])
        elif app == 1:
            delta.append(sums[first_row + 1 : first_row + 2])
            alpha0 = gamma[0] / delta[0]
            update(w1, w0, -alpha0, q0)
            for sub, part in owned:
                own = face(2 * part + 1)
                r1[sub, part] = r0[sub, own] - alpha0 * w0[sub, own]
        else:
            gamma.append(sums[first_row : first_row + 1])
            delta.append(sums[first_row + 1 : first_row + 2])

    beta1 = gamma[1] / gamma[0]
    alpha1 = gamma[1] / (delta[1] - beta1 * gamma[1] / alpha0)
    for sub, part in owned:
        own = face(2 * part + 1)
        z1 = q1[sub, own] + beta1 * q0[sub, own]
        s_value = w1[sub, own] + beta1 * w0[sub, own]
        p_value = r1[sub, part] + beta1 * r0[sub, own]
        s1[sub, part] = s_value
        p1[sub, part] = p_value
        x2[sub, part] = alpha0 * r0[sub, own] + alpha1 * p_value
        r2[sub, part] = r1[sub, part] - alpha1 * s_value
        w2[sub, part] = w1[sub, own] - alpha1 * z1

    sums = jnp.concatenate(
        [dot(plain(r2), plain(r2)), dot(plain(r2), plain(w2)), jnp.zeros((6, RHS), F32)], axis=0
    )
    base = 0
    for buffer, here, peers in (
        (s["end_y"], y, y_peers),
        (s["end_z"], z, z_peers),
        (s["end_x"], x, x_peers),
    ):
        buffer[here] = sums
        copies = [
            send(buffer.at[here], buffer.at[here], s["end_sem"], (base + d,), peer)
            for d, peer in enumerate(peers)
        ]
        base += len(peers)
        for copy in copies:
            copy.wait_recv()
        sums = jnp.sum(buffer[...], axis=0)
    s["end_out"][...] = sums
    send(s["end_out"], s["end_in"], s["end_sem"], (base,), (y, mate)).wait_recv()
    sums = sums + s["end_in"][...]
    gamma2, delta2 = sums[0:1], sums[1:2]
    beta2 = gamma2 / gamma[1]
    alpha2 = gamma2 / (delta2 - beta2 * gamma2 / alpha1)
    for sub, part in owned:
        mult_out[0, sub, part] = x2[sub, part] + alpha2 * (r2[sub, part] + beta2 * p1[sub, part])
        res_out[0, sub, part] = r2[sub, part] - alpha2 * (w2[sub, part] + beta2 * s1[sub, part])
    for copy in started:
        copy.wait_send()


def per_device(ny, nx, nz, gap_load, offsets, corner_map, flexibility, coupling, corner_rows):
    shapes = scratch(ny, nx, nz, corner_rows.shape[-1])
    vmem, smem = (pl.BlockSpec(memory_space=space) for space in (pltpu.VMEM, pltpu.SMEM))
    out = jax.ShapeDtypeStruct(gap_load.shape, F32)
    return pl.pallas_call(
        functools.partial(kernel, ny, nx, nz, tuple(shapes)),
        out_shape=(out, out),
        in_specs=[vmem, smem, smem, vmem, vmem, pl.BlockSpec(memory_space=pl.ANY)],
        out_specs=(vmem, vmem),
        scratch_shapes=list(shapes.values()),
        compiler_params=pltpu.CompilerParams(
            collective_id=0, has_side_effects=True, vmem_limit_bytes=60 * 1024 * 1024
        ),
    )(gap_load, offsets, corner_map, coupling, corner_rows, flexibility)


def solution(mesh):
    ny, nb = mesh.shape["cuts"], mesh.shape["blk"]
    nz = 8 if nb == 64 else 2
    nx = nb // (2 * nz)
    in_specs = (
        P("cuts", "blk", None, None, None),
        P("cuts", "blk", None),
        P("cuts", "blk", None),
        P("cuts", "blk", None, None),
        P("cuts", "blk", None, None),
        P("cuts", "blk", None, None),
    )
    out_specs = (P("cuts", "blk", None, None, None), P("cuts", "blk", None, None, None))
    return jax.shard_map(
        functools.partial(per_device, ny, nx, nz),
        mesh=mesh,
        in_specs=in_specs,
        out_specs=out_specs,
        check_vma=False,
    )
```

time: 1320 us -> 114 us (0.09)
  waiting for transfers between devices: 746 us -> 0 us
  blocking collectives: 382 us -> 0 us
  Pallas kernels: 0 us -> 106 us
  local copies, waits for them, and re-layouts: 68.4 us -> 6.93 us
  matrix products: 49.6 us -> 0 us
  starting transfers between devices: 27.4 us -> 0 us
  other arithmetic: 18.2 us -> 0 us
  between operations: 14.7 us -> 0.64 us
    psum x3 -> x0, waiting for transfers between devices: 733 us -> none  [per_device(): coarse = lax.psum(partial_value, ('cuts', 'blk'))]
    psum x5 -> x0, blocking collectives: 382 us -> none  [the longest x3 224 us: squares(): return lax.psum(inner_sum(residual, residual), ('cuts', 'blk'))]
    pallas_call x0 -> x1, Pallas kernels: none -> 106 us  [per_device(): pl.pallas_call(functools.partial(kernel, ny, nx, nz, tuple(shapes)), out_...]
    dot_general x12 -> x0, matrix products: 49.6 us -> none  [the longest x3 34.1 us: per_device(): moved = jnp.einsum('rcij,rcjn->rcin', flexibility, loads, precision=HIGH)]
    gather x12 -> x0, local copies, waits for them, and re-layouts: 43.9 us -> none  [rotate(): return jnp.take_along_axis(values, indices[..., None], axis=-2)]
    ppermute x12 -> x0, starting transfers between devices: 27.1 us -> none  [the longest x6 15.3 us: passed_along(): return lax.ppermute(value, axis, pairs)]
  transfers between devices with their start and end apart: 15 -> 0, of which waited for: 12 -> 0; matrix products, arithmetic and copies ran while one was open for 5% -> 0% of each run, Pallas kernels for 0% -> 0%
where the time goes in v1:
time: 114 us
  Pallas kernels  106 us (93%)
  local copies, waits for them, and re-layouts  6.93 us (6%)
    pallas_call x1, Pallas kernels, per_device(): pl.pallas_call(functools.partial(kernel, ny, nx, nz, tuple(shapes)), out_...  106 us
    unnamed x4, local copies, waits for them, and re-layouts  6.93 us

profile of v1, /device:TPU:1, one launch (start us, length us, event | category | flops | bytes accessed | tf_op | source)
XLA Modules:
  0.0 113.7 jit_solution(16189832566654676838)
XLA Ops:
  0.6 1.6 %copy.8.coup = f32[1,2,12,1024]{3,2,1,0:T(8,128)} copy(f32[1,2,12,1024]{3,1,2,0:T(2,128)} %param.10) | data formatting | bytes 196608 | tf_op args[4]
  2.2 1.6 %copy.9.rows = f32[1,2,12,1536]{3,2,1,0:T(8,128)} copy(f32[1,2,12,1536]{3,1,2,0:T(2,128)} %param.11) | data formatting | bytes 294912 | tf_op args[5]
  3.8 106.1 %shard_map.77 = (f32[1,2,2,256,128]{4,3,2,1,0:T(8,128)}, f32[1,2,2,256,128]{4,3,2,1,0:T(8,128)}) custom-call(f32[1,2,2,256,128]{4,3,2,1,0:T(8,128)} %gap.1, s32[1,2,2]{2,1,0:T(2,128)} %offs.1, s32[1,2,4]{2,1,0:T(2,128)} %cmap.1, f32[1,2,12,1024]{3,2,1,0:T(8,128)} %copy.8.coup, f32[1,2,12,1536]{3,2,1,0:T(8,128)} %copy.9.rows, f32[1,2,1024,1024]{3,2,1,0:T(8,128)} %flex.1), custom_call_target="tpu_custom_call" | custom-call | tf_op jit(solution)/shard_map/pallas_call | solution.py:519
  109.9 1.9 %copy.12 = f32[1,2,2,256,128]{4,3,2,1,0:T(8,128)} copy(f32[1,2,2,256,128]{4,3,2,1,0:T(8,128)} %get-tuple-element.4) | data formatting | bytes 1048576
  111.8 1.9 %copy.13 = f32[1,2,2,256,128]{4,3,2,1,0:T(8,128)} copy(f32[1,2,2,256,128]{4,3,2,1,0:T(8,128)} %get-tuple-element.5) | data formatting | bytes 1048576

commit v2 on v1

v2 whole, which is shorter than its diff:
```python
import functools
import types

import jax
import jax.numpy as jnp
from jax import lax
from jax.experimental import pallas as pl
from jax.experimental.pallas import tpu as pltpu
from jax.sharding import PartitionSpec as P

MESH = pl.DeviceIdType.MESH
F32, BF16 = jnp.float32, jnp.bfloat16
FD, RHS = 256, 128
NEAR, FAR, LEFT, RIGHT = 0, 1, 2, 3
BLOCK = 40
APPS = 3


def halves(value):
    high = value.astype(BF16)
    return high, (value - high.astype(F32)).astype(BF16)


def quadrants(product):
    rows = product.shape[0] // 2
    wide = product[:rows] + product[rows:]
    return wide[:, :RHS] + wide[:, RHS:]


def face(index):
    return slice(index * FD, (index + 1) * FD)


def scratch(ny, nx, nz, dofs):
    dma = pltpu.SemaphoreType.DMA
    rounds = APPS + 1
    return dict(
        gap=pltpu.VMEM((1, 2, 2, FD, RHS), F32),
        coup=pltpu.VMEM((12, 2, 4 * FD), F32),
        rows=pltpu.VMEM((12, 2, dofs), F32),
        offs=pltpu.SMEM((1, 2, 2), jnp.int32),
        cmap=pltpu.SMEM((1, 2, 4), jnp.int32),
        stage=pltpu.VMEM((4, FD, 4 * FD), F32),
        flex_parts=pltpu.VMEM((2, 2, 4 * FD, 4 * FD), BF16),
        info=pltpu.VMEM((8, 128), jnp.int32),
        info_near=pltpu.VMEM((8, 128), jnp.int32),
        info_left=pltpu.VMEM((8, 128), jnp.int32),
        word_near=pltpu.SMEM((8, 128), jnp.int32),
        word_left=pltpu.SMEM((8, 128), jnp.int32),
        coup_pad=pltpu.VMEM((128, 4 * FD), F32),
        coup_t=pltpu.VMEM((2, 4 * FD, 128), BF16),
        coup_t_n=pltpu.VMEM((6, FD, 128), BF16),
        coup_far=pltpu.VMEM((12, 2, FD), F32),
        coup_near=pltpu.VMEM((12, 2, FD), F32),
        coup_left=pltpu.VMEM((12, 2, FD), F32),
        coup_right=pltpu.VMEM((12, 2, FD), F32),
        node_pad=pltpu.VMEM((32, 4 * FD), F32),
        node_rows=pltpu.VMEM((2, 64, 4 * FD), BF16),
        rows_pad=pltpu.VMEM((24, dofs), F32),
        rows_parts=pltpu.VMEM((64, dofs), BF16),
        pick=pltpu.VMEM((nz * BLOCK, dofs), BF16),
        picked=pltpu.VMEM((nx, 2, 24, nz * BLOCK), F32),
        picked_in=pltpu.VMEM((nx, 2, 24, nz * BLOCK), F32),
        coarse=pltpu.VMEM((2 * nx * 48, nz * BLOCK), BF16),
        number_y=pltpu.VMEM((ny, 8, 128), F32),
        number_z=pltpu.VMEM((nz, 8, 128), F32),
        number_x=pltpu.VMEM((nx, 2, 8, 128), F32),
        line=pltpu.VMEM((APPS, ny, 32, RHS), F32),
        blocks=pltpu.VMEM((APPS, nz, BLOCK, RHS), F32),
        gap_near=pltpu.VMEM((2, FD, RHS), F32),
        gap_left=pltpu.VMEM((FD, RHS), F32),
        vec=pltpu.VMEM((5, 2, 4 * FD, RHS), F32),
        split=pltpu.VMEM((2, 4 * FD, 2 * RHS), BF16),
        moved=pltpu.VMEM((APPS, 2, 4 * FD, RHS), F32),
        total=pltpu.VMEM((2, 4 * FD, RHS), F32),
        face_far=pltpu.VMEM((APPS, 2, FD, RHS), F32),
        face_near=pltpu.VMEM((APPS, 2, FD, RHS), F32),
        face_left=pltpu.VMEM((APPS, FD, RHS), F32),
        face_right=pltpu.VMEM((APPS, FD, RHS), F32),
        twice=pltpu.VMEM((8, 2 * FD, RHS), F32),
        part_out=pltpu.VMEM((APPS, nx, 2, 32, RHS), F32),
        part_in=pltpu.VMEM((APPS, nx, 2, 32, RHS), F32),
        y_own=pltpu.VMEM((APPS, 2, 16, RHS), F32),
        y_far=pltpu.VMEM((APPS, 2, 16, RHS), F32),
        y_near=pltpu.VMEM((APPS, 2, 16, RHS), F32),
        y_left=pltpu.VMEM((APPS, 16, RHS), F32),
        y_right=pltpu.VMEM((APPS, 16, RHS), F32),
        own=pltpu.VMEM((6, 2, 2, FD, RHS), F32),
        end_y=pltpu.VMEM((ny, 8, RHS), F32),
        end_z=pltpu.VMEM((nz, 8, RHS), F32),
        end_x=pltpu.VMEM((nx, 2, 8, RHS), F32),
        stage_sem=dma((4,)),
        load_sem=dma((5,)),
        word_sem=dma((2,)),
        setup_sem=dma((2, 10)),
        y_sem=dma((2, rounds, ny - 1)),
        z_sem=dma((2, rounds, nz - 1)),
        x_sem=dma((2, rounds, 2 * nx - 1)),
        pick_sem=dma((2, 2 * nx - 1)),
        face_sem=dma((2, APPS, 4)),
        yv_sem=dma((2, APPS, 4)),
        end_sem=dma((2, ny + 2 * nx + nz - 3)),
    )


def kernel(ny, nx, nz, names, gap_in, offs_in, cmap_in, coup_in, rows_in, flex, mult_out, res_out, *refs):
    s = types.SimpleNamespace(**dict(zip(names, refs)))
    y, b = lax.axis_index("cuts"), lax.axis_index("blk")
    nb = 2 * nx * nz
    k = lax.rem(b, 2)
    z = lax.rem(b // 2, nz)
    x = b // (2 * nz)
    at = lambda xx, zz, kk: (xx * nz + zz) * 2 + kk
    up, down = lax.rem(y + 1, ny), lax.rem(y + ny - 1, ny)
    right, left = lax.rem(b + 1, nb), lax.rem(b + nb - 1, nb)
    y_peers = [(lax.rem(y + d, ny), b) for d in range(1, ny)]
    z_peers = [(y, at(x, lax.rem(z + d, nz), k)) for d in range(1, nz)]
    x_line = [(lax.rem(x + d, nx), lax.rem(k + e, 2)) for d in range(nx) for e in range(2)]
    x_peers = [(y, at(xx, z, kk)) for xx, kk in x_line[1:]]
    started = []

    def send(src, dst, sems, index, peer):
        copy = pltpu.make_async_remote_copy(
            src_ref=src,
            dst_ref=dst,
            send_sem=sems.at[(0,) + index],
            recv_sem=sems.at[(1,) + index],
            device_id=peer,
            device_id_type=MESH,
        )
        copy.start()
        started.append(copy)
        return copy

    greeted = y_peers + z_peers + x_peers + [(y, right), (y, left)]
    barrier = pltpu.get_barrier_semaphore()
    for peer in greeted:
        pl.semaphore_signal(barrier, inc=1, device_id=peer, device_id_type=MESH)

    loads = [
        pltpu.make_async_copy(source, getattr(s, name), s.load_sem.at[i])
        for i, (name, source) in enumerate(
            dict(cmap=cmap_in, offs=offs_in, gap=gap_in, coup=coup_in, rows=rows_in).items()
        )
    ]
    for copy in loads:
        copy.start()
    chunks = [(sub, 2 * group + part) for group in range(2) for sub in range(2) for part in range(2)]

    def fetch(chunk):
        sub, part = chunks[chunk]
        return pltpu.make_async_copy(
            flex.at[0, sub, face(part), :], s.stage.at[chunk % 4], s.stage_sem.at[chunk % 4]
        )

    for chunk in range(4):
        fetch(chunk).start()

    loads[0].wait()
    loads[1].wait()
    gap, offs, cmap, coup, rows = s.gap, s.offs, s.cmap, s.coup, s.rows

    lane = lax.broadcasted_iota(jnp.int32, (8, 128), 1) - 9 * y
    slot = jnp.where(lane < 3, 0, jnp.where(lane < 6, 1, 2))
    node = jnp.where(lane < 3, cmap[0, 0, 2], jnp.where(lane < 6, cmap[0, 1, 2], cmap[0, 1, 3]))
    here = (lane >= 0) & (lane < 9) & (lax.broadcasted_iota(jnp.int32, (8, 128), 0) == z)
    s.number_y[y] = jnp.where(here, 3 * node + lane - 3 * slot, 0).astype(F32)
    row8 = lax.broadcasted_iota(jnp.int32, (8, 128), 0)
    s.info[...] = jnp.where(row8 == 0, offs[0, 0, 0], jnp.where(row8 == 1, offs[0, 1, 0], offs[0, 1, 1]))

    pl.semaphore_wait(barrier, len(greeted))

    def to_all(buffer, sems, rd, peers):
        return [send(buffer, buffer, sems, (rd, d), peer) for d, peer in enumerate(peers)]

    number_copies = to_all(s.number_y.at[y], s.y_sem, 0, y_peers)
    setup = s.setup_sem
    got_gap_near = send(gap_in.at[0, :, 0], s.gap_near, setup, (0,), (up, b))
    got_gap_left = send(gap_in.at[0, 1, 1], s.gap_left, setup, (1,), (y, right))
    got_info_near = send(s.info, s.info_near, setup, (2,), (up, b))
    got_info_left = send(s.info, s.info_left, setup, (3,), (y, right))
    got_coup = [
        send(coup_in.at[:, :, face(NEAR)], s.coup_far, setup, (5,), (down, b)),
        send(coup_in.at[:, :, face(FAR)], s.coup_near, setup, (6,), (up, b)),
        send(coup_in.at[:, :, face(RIGHT)], s.coup_left, setup, (7,), (y, right)),
        send(coup_in.at[:, :, face(LEFT)], s.coup_right, setup, (8,), (y, left)),
    ]

    def unpack(target, first, matrix, sub):
        for i in range(12):
            target[first + i : first + i + 1, 0 : matrix.shape[2]] = matrix[i, sub : sub + 1]

    for copy in loads[2:]:
        copy.wait()
    not_first = jnp.where(y > 0, 1.0, 0.0).astype(F32)
    not_last = jnp.where(y < ny - 1, 1.0, 0.0).astype(F32)
    for sub in range(2):
        unpack(s.coup_pad, 0, coup, sub)
        s.node_pad[...] = jnp.zeros((32, 4 * FD), F32)
        s.node_pad[3 * sub : 3 * sub + 6] = s.coup_pad[6:12]
        s.node_pad[16 + 3 * sub : 22 + 3 * sub] = s.coup_pad[0:6] * not_first
        high, low = halves(s.node_pad[...])
        s.node_rows[sub, 0:32] = high
        s.node_rows[sub, 32:64] = low

    def transposed(matrix, sub):
        width = matrix.shape[2]
        pad = s.coup_pad
        unpack(pad, 0, matrix, sub)
        value = pad[0:12, 0:width]
        high = value.astype(BF16).astype(F32)
        low = value - high
        pad[:, 0:width] = jnp.zeros((128, width), F32)
        pad[0:12, 0:width] = high
        pad[16:28, 0:width] = low
        pad[32:44, 0:width] = high
        pad[48:60, 0:width] = low
        return pad[:, 0:width].T.astype(BF16)

    for sub in range(2):
        s.coup_t[sub] = transposed(coup, sub)

    def make_block():
        own = s.blocks.at[app, z]
        for cycle in range(ny):
            value = s.line[app, cycle, 0:9]
            if cycle + 1 < ny:
                value = value + s.line[app, cycle + 1, 16:25]
            own[9 * cycle : 9 * cycle + 9] = value
        sums = s.line[app, 0, 9:13]
        for cycle in range(1, ny):
            sums = sums + s.line[app, cycle, 9:13]
        own[9 * ny : 9 * ny + 4] = sums

    for copy in number_copies:
        copy.wait_recv()
    s.number_z[z] = jnp.sum(s.number_y[...], axis=0)
    number_copies = to_all(s.number_z.at[z], s.z_sem, 0, z_peers)

    def rolled(index, value, start):
        s.twice[index, 0:FD] = value
        s.twice[index, FD : 2 * FD] = value
        return s.twice[index, pl.ds(start, FD)]

    ahead = lambda off: lax.rem(off + FD, FD)
    back = lambda off: lax.rem(FD - off, FD)
    on = lambda off: jnp.where(off >= 0, 1.0, 0.0).astype(F32)
    got_info_near.wait_recv()
    got_info_left.wait_recv()
    words = [
        pltpu.make_async_copy(s.info_near, s.word_near, s.word_sem.at[0]),
        pltpu.make_async_copy(s.info_left, s.word_left, s.word_sem.at[1]),
    ]
    for copy in words:
        copy.start()
    for copy in words:
        copy.wait()
    off_far = [offs[0, sub, 0] for sub in range(2)]
    off_right = [offs[0, sub, 1] for sub in range(2)]
    off_near = [s.word_near[sub, 0] for sub in range(2)]
    off_left = s.word_left[2, 0]
    on_far = [on(off) for off in off_far]
    on_right = [on(off) for off in off_right]
    on_near = [on(off) * not_first for off in off_near]
    on_left = on(off_left)

    def convert(turn):
        sub, part = chunks[turn]
        fetch(turn).wait()

        @pl.loop(0, FD // 64)
        def _(step):
            at_row = pl.multiple_of(step * 64, 64)
            high, low = halves(s.stage[turn % 4, pl.ds(at_row, 64)])
            base = FD * (part % 2)
            s.flex_parts[sub, part // 2, pl.ds(base + at_row, 64)] = high
            s.flex_parts[sub, part // 2, pl.ds(2 * FD + base + at_row, 64)] = low

        if turn + 4 < 8:
            fetch(turn + 4).start()

    for turn in range(4):
        convert(turn)

    for copy in number_copies:
        copy.wait_recv()
    s.number_x[x, k] = jnp.sum(s.number_z[...], axis=0)
    number_copies = to_all(s.number_x.at[x, k], s.x_sem, 0, x_peers)

    for sub in range(2):
        unpack(s.rows_pad, 12 * sub, rows, sub)
    high, low = halves(jnp.concatenate([s.rows_pad[...], jnp.zeros((8, rows.shape[2]), F32)], axis=0))
    s.rows_parts[0:32] = high
    s.rows_parts[32:64] = low
    s.y_own[...] = jnp.zeros(s.y_own.shape, F32)

    got_gap_near.wait_recv()
    got_gap_left.wait_recv()
    r0, w0, q0, w1, q1 = (s.vec.at[i] for i in range(5))
    for sub in range(2):
        r0[sub, face(FAR)] = gap[0, sub, 0] * on_far[sub]
        r0[sub, face(RIGHT)] = gap[0, sub, 1] * on_right[sub]
        r0[sub, face(NEAR)] = rolled(sub, s.gap_near[sub], ahead(off_near[sub])) * -on_near[sub]
    r0[0, face(LEFT)] = rolled(2, s.gap_left[...], ahead(off_left)) * -on_left
    r0[1, face(LEFT)] = rolled(3, gap[0, 0, 1], ahead(off_right[0])) * -on_right[0]

    owned = [(sub, part) for sub in range(2) for part in range(2)]

    def dot(first, second):
        total = None
        for sub, part in owned:
            term = jnp.sum(first(sub, part) * second(sub, part), axis=0, keepdims=True)
            total = term if total is None else total + term
        return total

    def of(vector):
        return lambda sub, part: vector[sub, face(2 * part + 1)]

    def product(sub, group):
        wide = jnp.dot(s.flex_parts[sub, group], s.split[sub], preferred_element_type=F32)
        s.moved[app, sub, 2 * FD * group : 2 * FD * (group + 1)] = quadrants(wide)

    def stacked(value):
        high, low = halves(value)
        return jnp.concatenate([high, high, low, low, jnp.zeros((64, RHS), BF16)], axis=0)

    def begin(vector, dots):
        for sub in range(2):
            high, low = halves(vector[sub])
            s.split[sub, :, 0:RHS] = high
            s.split[sub, :, RHS : 2 * RHS] = low
        wide = jnp.dot(s.node_rows[0], s.split[0], preferred_element_type=F32)
        wide = wide + jnp.dot(s.node_rows[1], s.split[1], preferred_element_type=F32)
        tile = s.line.at[app, y]
        tile[...] = quadrants(wide)
        tile[9:11] = jnp.concatenate(dots, axis=0)
        return to_all(tile, s.y_sem, app + 1, y_peers)

    def finish_faces(result, last):
        moved = s.total
        for sub in range(2):
            term = jnp.dot(s.coup_t[sub], stacked(s.y_own[app, sub]), preferred_element_type=F32)
            moved[sub] = s.moved[app, sub] + term

        def other(index, value, y_value):
            return value + jnp.dot(s.coup_t_n[index], stacked(y_value), preferred_element_type=F32)

        inner_left, inner_right = moved[1, face(LEFT)], moved[0, face(RIGHT)]
        result[0, face(RIGHT)] = (inner_right - rolled(0, inner_left, back(off_right[0]))) * on_right[0]
        if not last:
            result[1, face(LEFT)] = (inner_left - rolled(1, inner_right, ahead(off_right[0]))) * on_right[0]
        for copy in got_y:
            copy.wait_recv()
        for copy in got_faces:
            copy.wait_recv()
        for sub in range(2):
            value = other(sub, s.face_far[app, sub], s.y_far[app, sub]) * not_last
            jump = moved[sub, face(FAR)] - rolled(2 + sub, value, back(off_far[sub]))
            result[sub, face(FAR)] = jump * on_far[sub]
            if not last:
                value = other(2 + sub, s.face_near[app, sub], s.y_near[app, sub])
                jump = moved[sub, face(NEAR)] - rolled(4 + sub, value, ahead(off_near[sub]))
                result[sub, face(NEAR)] = jump * on_near[sub]
        value = other(5, s.face_right[app], s.y_right[app])
        jump = moved[1, face(RIGHT)] - rolled(6, value, back(off_right[1]))
        result[1, face(RIGHT)] = jump * on_right[1]
        if not last:
            value = other(4, s.face_left[app], s.y_left[app])
            jump = moved[0, face(LEFT)] - rolled(7, value, ahead(off_left))
            result[0, face(LEFT)] = jump * on_left

    def update(target, base, factor, step):
        for sub in range(2):
            for part in range(4):
                target[sub, face(part)] = base[sub, face(part)] + factor * step[sub, face(part)]

    none = jnp.zeros((1, RHS), F32)
    r1, p1, x2, r2, s1, w2 = (s.own.at[i] for i in range(6))
    plain = lambda vector: lambda sub, part: vector[sub, part]
    gamma, delta = [], []
    for app in range(APPS):
        last = app == APPS - 1
        if app == 0:
            vector, result, dots = r0, w0, [dot(of(r0), of(r0)), none]
        elif app == 1:
            vector, result, dots = w0, q0, [none, dot(of(r0), of(w0))]
        else:
            vector, result = w1, q1
            dots = [dot(plain(r1), plain(r1)), dot(plain(r1), of(w1))]
        got_line = begin(vector, dots)
        moved = s.moved.at[app]
        for sub in range(2):
            product(sub, 0)
        got_faces = [send(moved.at[:, face(NEAR)], s.face_far.at[app], s.face_sem, (app, 0), (down, b))]
        if not last:
            got_faces.append(
                send(moved.at[:, face(FAR)], s.face_near.at[app], s.face_sem, (app, 1), (up, b))
            )
        for copy in got_line:
            copy.wait_recv()
        make_block()
        got_z = to_all(s.blocks.at[app, z], s.z_sem, app + 1, z_peers)
        if app == 0:
            for turn in range(4, 8):
                convert(turn)
        for sub in range(2):
            product(sub, 1)
        got_faces.append(
            send(moved.at[0, face(LEFT)], s.face_right.at[app], s.face_sem, (app, 2), (y, left))
        )
        if not last:
            got_faces.append(
                send(moved.at[1, face(RIGHT)], s.face_left.at[app], s.face_sem, (app, 3), (y, right))
            )
        if app == 0:
            for copy in number_copies:
                copy.wait_recv()
            dofs = s.pick.shape[1]
            lane = lax.broadcasted_iota(jnp.int32, (8, 128), 1)
            got_picked = []
            for i, (xx, kk) in enumerate(x_line):
                tile = jnp.where(lane < 9 * ny, s.number_x[xx, kk], -1.0)
                column = jnp.concatenate([tile, jnp.zeros((120, 128), F32)], axis=0).T
                numbers = jnp.concatenate(
                    [jnp.broadcast_to(column[0:BLOCK, j : j + 1], (BLOCK, 128)) for j in range(nz)], axis=0
                )
                for q in range(dofs // 128):
                    wanted = (lax.broadcasted_iota(jnp.int32, numbers.shape, 1) + 128 * q).astype(F32)
                    s.pick[:, 128 * q : 128 * q + 128] = jnp.where(numbers == wanted, 1.0, 0.0).astype(BF16)
                both = lax.dot_general(
                    s.rows_parts[...],
                    s.pick[...],
                    (((1,), (1,)), ((), ())),
                    preferred_element_type=F32,
                )
                own_rows = both[0:24] + both[32:56]
                if i == 0:
                    s.picked_in[x, k] = own_rows
                else:
                    s.picked[xx, kk] = own_rows
                    got_picked.append(
                        send(s.picked.at[xx, kk], s.picked_in.at[x, k], s.pick_sem, (i - 1,), x_peers[i - 1])
                    )
            for copy in got_coup:
                copy.wait_recv()
            for sub in range(2):
                s.coup_t_n[sub] = transposed(s.coup_far, sub)
                s.coup_t_n[2 + sub] = transposed(s.coup_near, sub)
            s.coup_t_n[4] = transposed(s.coup_left, 1)
            s.coup_t_n[5] = transposed(s.coup_right, 0)
            for copy in got_picked:
                copy.wait_recv()
            for i in range(2 * nx):
                high, low = halves(s.picked_in[i // 2, i % 2])
                s.coarse[24 * i : 24 * i + 24] = high
                s.coarse[48 * nx + 24 * i : 48 * nx + 24 * i + 24] = low
        for copy in got_z:
            copy.wait_recv()
        loads = s.blocks[app]
        sums = jnp.sum(loads[:, BLOCK - 8 :, :], axis=0)
        high, low = halves(loads.reshape(nz * BLOCK, RHS))
        wide = jnp.dot(s.coarse[...], jnp.concatenate([high, low], axis=1), preferred_element_type=F32)
        parts = quadrants(wide)
        for i in range(2 * nx):
            s.part_out[app, i // 2, i % 2, 0:24] = parts[24 * i : 24 * i + 24]
            s.part_out[app, i // 2, i % 2, 24:32] = sums
        got_parts = []
        for i, (xx, kk) in enumerate(x_line):
            if i == 0:
                s.part_in[app, x, k] = s.part_out[app, x, k]
            else:
                got_parts.append(
                    send(
                        s.part_out.at[app, xx, kk],
                        s.part_in.at[app, x, k],
                        s.x_sem,
                        (app + 1, i - 1),
                        x_peers[i - 1],
                    )
                )
        for copy in got_parts:
            copy.wait_recv()
        ysum = s.part_in[app, 0, 0]
        for i in range(1, 2 * nx):
            ysum = ysum + s.part_in[app, i // 2, i % 2]
        sums = ysum[24:32]
        for sub in range(2):
            s.y_own[app, sub, 0:12] = ysum[12 * sub : 12 * sub + 12]
        y_own = s.y_own.at[app]
        got_y = [
            send(y_own, s.y_far.at[app], s.yv_sem, (app, 0), (down, b)),
            send(y_own.at[0], s.y_right.at[app], s.yv_sem, (app, 2), (y, left)),
        ]
        if not last:
            got_y += [
                send(y_own, s.y_near.at[app], s.yv_sem, (app, 1), (up, b)),
                send(y_own.at[1], s.y_left.at[app], s.yv_sem, (app, 3), (y, right)),
            ]
        finish_faces(result, last)
        first_row = 9 * ny - (BLOCK - 8)
        if app == 0:
            gamma.append(sums[first_row : first_row + 1])
        elif app == 1:
            delta.append(sums[first_row + 1 : first_row + 2])
            alpha0 = gamma[0] / delta[0]
            update(w1, w0, -alpha0, q0)
            for sub, part in owned:
                own = face(2 * part + 1)
                r1[sub, part] = r0[sub, own] - alpha0 * w0[sub, own]
        else:
            gamma.append(sums[first_row : first_row + 1])
            delta.append(sums[first_row + 1 : first_row + 2])

    beta1 = gamma[1] / gamma[0]
    alpha1 = gamma[1] / (delta[1] - beta1 * gamma[1] / alpha0)
    for sub, part in owned:
        own = face(2 * part + 1)
        z1 = q1[sub, own] + beta1 * q0[sub, own]
        s_value = w1[sub, own] + beta1 * w0[sub, own]
        p_value = r1[sub, part] + beta1 * r0[sub, own]
        s1[sub, part] = s_value
        p1[sub, part] = p_value
        x2[sub, part] = alpha0 * r0[sub, own] + alpha1 * p_value
        r2[sub, part] = r1[sub, part] - alpha1 * s_value
        w2[sub, part] = w1[sub, own] - alpha1 * z1

    sums = jnp.concatenate(
        [dot(plain(r2), plain(r2)), dot(plain(r2), plain(w2)), jnp.zeros((6, RHS), F32)], axis=0
    )
    base = 0
    for buffer, here, peers in (
        (s.end_y, (y,), y_peers),
        (s.end_z, (z,), z_peers),
        (s.end_x, (x, k), x_peers),
    ):
        buffer[here] = sums
        copies = [
            send(buffer.at[here], buffer.at[here], s.end_sem, (base + d,), peer)
            for d, peer in enumerate(peers)
        ]
        base += len(peers)
        for copy in copies:
            copy.wait_recv()
        sums = jnp.sum(buffer[...], axis=tuple(range(len(here))))
    gamma2, delta2 = sums[0:1], sums[1:2]
    beta2 = gamma2 / gamma[1]
    alpha2 = gamma2 / (delta2 - beta2 * gamma2 / alpha1)
    for sub, part in owned:
        mult_out[0, sub, part] = x2[sub, part] + alpha2 * (r2[sub, part] + beta2 * p1[sub, part])
        res_out[0, sub, part] = r2[sub, part] - alpha2 * (w2[sub, part] + beta2 * s1[sub, part])
    for copy in started:
        copy.wait_send()


def hand_on(mult_in, res_in, mult_out, res_out):
    mult_out[...] = mult_in[...]
    res_out[...] = res_in[...]


def per_device(ny, nx, nz, gap_load, offsets, corner_map, flexibility, coupling, corner_rows):
    shapes = scratch(ny, nx, nz, corner_rows.shape[-1])
    vmem, hbm = (pl.BlockSpec(memory_space=space) for space in (pltpu.VMEM, pltpu.HBM))
    out = jax.ShapeDtypeStruct(gap_load.shape, F32)

    results = pl.pallas_call(
        functools.partial(kernel, ny, nx, nz, tuple(shapes)),
        out_shape=(out, out),
        in_specs=[hbm] * 6,
        out_specs=(vmem, vmem),
        scratch_shapes=list(shapes.values()),
        compiler_params=pltpu.CompilerParams(
            collective_id=0, has_side_effects=True, vmem_limit_bytes=60 * 1024 * 1024
        ),
    )(gap_load, offsets, corner_map, coupling[0].transpose(1, 0, 2), corner_rows[0].transpose(1, 0, 2), flexibility)
    return pl.pallas_call(
        hand_on, out_shape=(out, out), in_specs=[vmem, vmem], out_specs=(vmem, vmem)
    )(*results)


def solution(mesh):
    ny, nb = mesh.shape["cuts"], mesh.shape["blk"]
    nz = 8 if nb == 64 else 2
    nx = nb // (2 * nz)
    in_specs = (
        P("cuts", "blk", None, None, None),
        P("cuts", "blk", None),
        P("cuts", "blk", None),
        P("cuts", "blk", None, None),
        P("cuts", "blk", None, None),
        P("cuts", "blk", None, None),
    )
    out_specs = (P("cuts", "blk", None, None, None), P("cuts", "blk", None, None, None))
    return jax.shard_map(
        functools.partial(per_device, ny, nx, nz),
        mesh=mesh,
        in_specs=in_specs,
        out_specs=out_specs,
        check_vma=False,
    )
```

time: 114 us -> 98.6 us (0.86)
  Pallas kernels: 106 us -> 97.9 us
  local copies, waits for them, and re-layouts: 6.93 us -> 0 us
    pallas_call x1, Pallas kernels: 106 us -> 95.7 us  [per_device(): pl.pallas_call(functools.partial(kernel, ny, nx, nz, tuple(shapes)), out_...]
    unnamed x4 -> x0, local copies, waits for them, and re-layouts: 6.93 us -> none
    pallas_call x0 -> x1, Pallas kernels: none -> 2.2 us  [per_device(): pl.pallas_call(hand_on, out_shape=(out, out), in_specs=[vmem, vmem], out_...]
where the time goes in v2:
time: 98.6 us; the launch traced here: 98.5 us
  Pallas kernels  97.9 us (99%)
    pallas_call x1, Pallas kernels, per_device(): pl.pallas_call(functools.partial(kernel, ny, nx, nz, tuple(shapes)), out_...  95.7 us
    pallas_call x1, Pallas kernels, per_device(): pl.pallas_call(hand_on, out_shape=(out, out), in_specs=[vmem, vmem], out_...  2.2 us

profile of v2, /device:TPU:1, one launch (start us, length us, event | category | flops | bytes accessed | tf_op | source)
XLA Modules:
  0.0 98.5 jit_solution(6936579199363327829)
XLA Ops:
  0.6 95.7 %shard_map.77 = (f32[1,2,2,256,128]{4,3,2,1,0:T(8,128)}, f32[1,2,2,256,128]{4,3,2,1,0:T(8,128)}) custom-call(f32[1,2,2,256,128]{4,3,2,1,0:T(8,128)} %gap_in.1, s32[1,2,2]{2,1,0:T(2,128)} %offs_in.1, s32[1,2,4]{2,1,0:T(2,128)} %cmap_in.1, f32[12,2,1024]{2,1,0:T(2,128)} %bitcast.7, f32[12,2,1536]{2,1,0:T(2,128)} %bitcast.6, f32[1,2,1024,1024]{3,2,1,0:T(8,128)} %flex.1), custom_call_target="tpu_custom_call" | custom-call | tf_op jit(solution)/shard_map/pallas_call | solution.py:565
  96.3 2.2 %shard_map.78 = (f32[1,2,2,256,128]{4,3,2,1,0:T(8,128)}, f32[1,2,2,256,128]{4,3,2,1,0:T(8,128)}) custom-call(f32[1,2,2,256,128]{4,3,2,1,0:T(8,128)} %get-tuple-element.4.mult_in, f32[1,2,2,256,128]{4,3,2,1,0:T(8,128)} %get-tuple-element.5.res_in), custom_call_target="tpu_custom_call" | custom-call | tf_op jit(solution)/shard_map/pallas_call | solution.py:575

commit v3 on v2

--- a/solution.py
+++ b/solution.py
@@ -40,7 +40,7 @@
         rows=pltpu.VMEM((12, 2, dofs), F32),
         offs=pltpu.SMEM((1, 2, 2), jnp.int32),
         cmap=pltpu.SMEM((1, 2, 4), jnp.int32),
-        stage=pltpu.VMEM((4, FD, 4 * FD), F32),
+        stage=pltpu.VMEM((8, FD, 4 * FD), F32),
         flex_parts=pltpu.VMEM((2, 2, 4 * FD, 4 * FD), BF16),
         info=pltpu.VMEM((8, 128), jnp.int32),
         info_near=pltpu.VMEM((8, 128), jnp.int32),
@@ -89,7 +89,7 @@
         end_y=pltpu.VMEM((ny, 8, RHS), F32),
         end_z=pltpu.VMEM((nz, 8, RHS), F32),
         end_x=pltpu.VMEM((nx, 2, 8, RHS), F32),
-        stage_sem=dma((4,)),
+        stage_sem=dma((8,)),
         load_sem=dma((5,)),
         word_sem=dma((2,)),
         setup_sem=dma((2, 10)),
@@ -113,9 +113,10 @@
     at = lambda xx, zz, kk: (xx * nz + zz) * 2 + kk
     up, down = lax.rem(y + 1, ny), lax.rem(y + ny - 1, ny)
     right, left = lax.rem(b + 1, nb), lax.rem(b + nb - 1, nb)
-    y_peers = [(lax.rem(y + d, ny), b) for d in range(1, ny)]
-    z_peers = [(y, at(x, lax.rem(z + d, nz), k)) for d in range(1, nz)]
-    x_line = [(lax.rem(x + d, nx), lax.rem(k + e, 2)) for d in range(nx) for e in range(2)]
+    far_first = lambda n: sorted(range(1, n), key=lambda d: -min(d, n - d))
+    y_peers = [(lax.rem(y + d, ny), b) for d in far_first(ny)]
+    z_peers = [(y, at(x, lax.rem(z + d, nz), k)) for d in far_first(nz)]
+    x_line = [(lax.rem(x + d, nx), lax.rem(k + e, 2)) for d in [0] + far_first(nx) for e in range(2)]
     x_peers = [(y, at(xx, z, kk)) for xx, kk in x_line[1:]]
     started = []
 
@@ -150,10 +151,10 @@
     def fetch(chunk):
         sub, part = chunks[chunk]
         return pltpu.make_async_copy(
-            flex.at[0, sub, face(part), :], s.stage.at[chunk % 4], s.stage_sem.at[chunk % 4]
+            flex.at[0, sub, face(part), :], s.stage.at[chunk], s.stage_sem.at[chunk]
         )
 
-    for chunk in range(4):
+    for chunk in range(8):
         fetch(chunk).start()
 
     loads[0].wait()
@@ -271,15 +272,12 @@
         @pl.loop(0, FD // 64)
         def _(step):
             at_row = pl.multiple_of(step * 64, 64)
-            high, low = halves(s.stage[turn % 4, pl.ds(at_row, 64)])
+            high, low = halves(s.stage[turn, pl.ds(at_row, 64)])
             base = FD * (part % 2)
             s.flex_parts[sub, part // 2, pl.ds(base + at_row, 64)] = high
             s.flex_parts[sub, part // 2, pl.ds(2 * FD + base + at_row, 64)] = low
 
-        if turn + 4 < 8:
-            fetch(turn + 4).start()
-
-    for turn in range(4):
+    for turn in range(8):
         convert(turn)
 
     for copy in number_copies:
@@ -374,6 +372,36 @@
             for part in range(4):
                 target[sub, face(part)] = base[sub, face(part)] + factor * step[sub, face(part)]
 
+    got_picked = []
+
+    def pick(first, stop):
+        dofs = s.pick.shape[1]
+        lane = lax.broadcasted_iota(jnp.int32, (8, 128), 1)
+        for i in range(first, stop):
+            xx, kk = x_line[i]
+            tile = jnp.where(lane < 9 * ny, s.number_x[xx, kk], -1.0)
+            column = jnp.concatenate([tile, jnp.zeros((120, 128), F32)], axis=0).T
+            numbers = jnp.concatenate(
+                [jnp.broadcast_to(column[0:BLOCK, j : j + 1], (BLOCK, 128)) for j in range(nz)], axis=0
+            )
+            for q in range(dofs // 128):
+                wanted = (lax.broadcasted_iota(jnp.int32, numbers.shape, 1) + 128 * q).astype(F32)
+                s.pick[:, 128 * q : 128 * q + 128] = jnp.where(numbers == wanted, 1.0, 0.0).astype(BF16)
+            both = lax.dot_general(
+                s.rows_parts[...],
+                s.pick[...],
+                (((1,), (1,)), ((), ())),
+                preferred_element_type=F32,
+            )
+            own_rows = both[0:24] + both[32:56]
+            if i == 0:
+                s.picked_in[x, k] = own_rows
+            else:
+                s.picked[xx, kk] = own_rows
+                got_picked.append(
+                    send(s.picked.at[xx, kk], s.picked_in.at[x, k], s.pick_sem, (i - 1,), x_peers[i - 1])
+                )
+
     none = jnp.zeros((1, RHS), F32)
     r1, p1, x2, r2, s1, w2 = (s.own.at[i] for i in range(6))
     plain = lambda vector: lambda sub, part: vector[sub, part]
@@ -389,20 +417,26 @@
             dots = [dot(plain(r1), plain(r1)), dot(plain(r1), of(w1))]
         got_line = begin(vector, dots)
         moved = s.moved.at[app]
-        for sub in range(2):
-            product(sub, 0)
+        if app == 0:
+            for copy in number_copies:
+                copy.wait_recv()
+            pick(0, nx)
+        else:
+            for sub in range(2):
+                product(sub, 0)
+        for copy in got_line:
+            copy.wait_recv()
+        make_block()
+        got_z = to_all(s.blocks.at[app, z], s.z_sem, app + 1, z_peers)
+        if app == 0:
+            pick(nx, 2 * nx)
+            for sub in range(2):
+                product(sub, 0)
         got_faces = [send(moved.at[:, face(NEAR)], s.face_far.at[app], s.face_sem, (app, 0), (down, b))]
         if not last:
             got_faces.append(
                 send(moved.at[:, face(FAR)], s.face_near.at[app], s.face_sem, (app, 1), (up, b))
             )
-        for copy in got_line:
-            copy.wait_recv()
-        make_block()
-        got_z = to_all(s.blocks.at[app, z], s.z_sem, app + 1, z_peers)
-        if app == 0:
-            for turn in range(4, 8):
-                convert(turn)
         for sub in range(2):
             product(sub, 1)
         got_faces.append(
@@ -413,34 +447,6 @@
                 send(moved.at[1, face(RIGHT)], s.face_left.at[app], s.face_sem, (app, 3), (y, right))
             )
         if app == 0:
-            for copy in number_copies:
-                copy.wait_recv()
-            dofs = s.pick.shape[1]
-            lane = lax.broadcasted_iota(jnp.int32, (8, 128), 1)
-            got_picked = []
-            for i, (xx, kk) in enumerate(x_line):
-                tile = jnp.where(lane < 9 * ny, s.number_x[xx, kk], -1.0)
-                column = jnp.concatenate([tile, jnp.zeros((120, 128), F32)], axis=0).T
-                numbers = jnp.concatenate(
-                    [jnp.broadcast_to(column[0:BLOCK, j : j + 1], (BLOCK, 128)) for j in range(nz)], axis=0
-                )
-                for q in range(dofs // 128):
-                    wanted = (lax.broadcasted_iota(jnp.int32, numbers.shape, 1) + 128 * q).astype(F32)
-                    s.pick[:, 128 * q : 128 * q + 128] = jnp.where(numbers == wanted, 1.0, 0.0).astype(BF16)
-                both = lax.dot_general(
-                    s.rows_parts[...],
-                    s.pick[...],
-                    (((1,), (1,)), ((), ())),
-                    preferred_element_type=F32,
-                )
-                own_rows = both[0:24] + both[32:56]
-                if i == 0:
-                    s.picked_in[x, k] = own_rows
-                else:
-                    s.picked[xx, kk] = own_rows
-                    got_picked.append(
-                        send(s.picked.at[xx, kk], s.picked_in.at[x, k], s.pick_sem, (i - 1,), x_peers[i - 1])
-                    )
             for copy in got_coup:
                 copy.wait_recv()
             for sub in range(2):

time: 98.6 us -> 93.8 us (0.951)
  Pallas kernels: 97.9 us -> 93 us
    pallas_call x1, Pallas kernels: 95.7 us -> 90.8 us  [per_device(): pl.pallas_call(functools.partial(kernel, ny, nx, nz, tuple(shapes)), out_...]
where the time goes in v3:
time: 93.8 us; the launch traced here: 93.7 us
  Pallas kernels  93 us (99%)
    pallas_call x1, Pallas kernels, per_device(): pl.pallas_call(functools.partial(kernel, ny, nx, nz, tuple(shapes)), out_...  90.8 us
    pallas_call x1, Pallas kernels, per_device(): pl.pallas_call(hand_on, out_shape=(out, out), in_specs=[vmem, vmem], out_...  2.2 us

profile of v3, /device:TPU:1, one launch (start us, length us, event | category | flops | bytes accessed | tf_op | source)
XLA Modules:
  0.0 93.7 jit_solution(16387017364264846363)
XLA Ops:
  0.6 90.8 %shard_map.77 = (f32[1,2,2,256,128]{4,3,2,1,0:T(8,128)}, f32[1,2,2,256,128]{4,3,2,1,0:T(8,128)}) custom-call(f32[1,2,2,256,128]{4,3,2,1,0:T(8,128)} %gap_in.1, s32[1,2,2]{2,1,0:T(2,128)} %offs_in.1, s32[1,2,4]{2,1,0:T(2,128)} %cmap_in.1, f32[12,2,1024]{2,1,0:T(2,128)} %bitcast.7, f32[12,2,1536]{2,1,0:T(2,128)} %bitcast.6, f32[1,2,1024,1024]{3,2,1,0:T(8,128)} %flex.1), custom_call_target="tpu_custom_call" | custom-call | tf_op jit(solution)/shard_map/pallas_call | solution.py:571
  91.5 2.2 %shard_map.78 = (f32[1,2,2,256,128]{4,3,2,1,0:T(8,128)}, f32[1,2,2,256,128]{4,3,2,1,0:T(8,128)}) custom-call(f32[1,2,2,256,128]{4,3,2,1,0:T(8,128)} %get-tuple-element.4.mult_in, f32[1,2,2,256,128]{4,3,2,1,0:T(8,128)} %get-tuple-element.5.res_in), custom_call_target="tpu_custom_call" | custom-call | tf_op jit(solution)/shard_map/pallas_call | solution.py:581
